TPU v7x, 256 devices: a whole 4x4x8 slice. The times are simulated.
256 devices in a mesh: row: 16 (over x_hi, y, core), col: 16 (over z, x_lo).
Axes of the slice: x: 4 (x_hi: 2, x_lo: 2; x = x_hi * 2 + x_lo), y: 4, z: 8, core: 2. Of those that a mesh axis runs over, the one named last changes fastest.
Arguments:
- inputs: bfloat16 [2048, 4096], P('row', 'col'), may hold values from -6 to 6
- grad_output: bfloat16 [2048, 4096], P('row', 'col'), may hold values from -6 to 6
- gate_pre: bfloat16 [2048, 14336], P('col', 'row'), may hold values from -6 to 6
- up_pre: bfloat16 [2048, 14336], P('col', 'row'), may hold values from -6 to 6
- gate_weight: bfloat16 [14336, 4096], P('row', 'col'), may hold values from -0.09375 to 0.09375
- up_weight: bfloat16 [14336, 4096], P('row', 'col'), may hold values from -0.09375 to 0.09375
- down_weight: bfloat16 [14336, 4096], P('row', 'col'), may hold values from -0.046875 to 0.046875
Outputs:
- grad_input: float32 [2048, 4096], P('row', 'col')
- grad_gate_weight: float32 [14336, 4096], P('row', 'col')
- grad_up_weight: float32 [14336, 4096], P('row', 'col')
- grad_down_weight: float32 [14336, 4096], P('row', 'col')
All inputs are finite; a program needn't handle non-finite values.
Results may differ from a plain program's by a relative error of at most 0.0029.
Values may be sent and summed in bfloat16 or wider, within the bound.
No kernel may reach another device: no remote copies, remote signals or barrier semaphores. Data moves between devices by JAX's collectives and lax.ppermute only.
A program may use at most 64 MiB of HBM per device.

v0:
```python
import math
import jax
import jax.numpy as jnp
from jax import lax
from jax.sharding import PartitionSpec as P


def outer_sum(left_rows, right_rows):
    return lax.dot_general(
        left_rows, right_rows, (((0,), (0,)), ((), ())), preferred_element_type=jnp.float32
    )


def inner_last(left_rows, right_rows):
    return lax.dot_general(
        left_rows, right_rows, (((1,), (1,)), ((), ())), preferred_element_type=jnp.float32
    )


def shards(inputs, grad_output, gate_pre, up_pre, gate_weight, up_weight, down_weight):
    input_cols, output_cols = (
        lax.all_gather(inputs, "row", axis=0, tiled=True),
        lax.all_gather(grad_output, "row", axis=0, tiled=True),
    )
    gate_value = gate_pre.astype(jnp.float32)
    up_value = up_pre.astype(jnp.float32)
    sigmoid_gate = jax.nn.sigmoid(gate_value)
    silu_gate = gate_value * sigmoid_gate
    hidden = (silu_gate * up_value).astype(jnp.bfloat16)
    output_rows = output_cols
    grad_hidden = lax.psum_scatter(
        inner_last(output_rows, down_weight), "col", scatter_dimension=0, tiled=True
    )
    grad_gate_pre = (
        grad_hidden * up_value * sigmoid_gate * (1.0 + gate_value * (1.0 - sigmoid_gate))
    ).astype(jnp.bfloat16)
    grad_up_pre = (grad_hidden * silu_gate).astype(jnp.bfloat16)
    gate_piece = lax.all_gather(grad_gate_pre, "col", axis=0, tiled=True)
    up_piece = lax.all_gather(grad_up_pre, "col", axis=0, tiled=True)
    gate_running = outer_sum(gate_piece, input_cols)
    up_running = outer_sum(up_piece, input_cols)
    input_part = jnp.dot(gate_piece, gate_weight, preferred_element_type=jnp.float32) + jnp.dot(
        up_piece, up_weight, preferred_element_type=jnp.float32
    )
    partial_input = input_part
    first_three = (gate_running, up_running, partial_input)
    output_rows = output_cols
    grad_gate, grad_up, partial_input, grad_down = first_three + (
        outer_sum(lax.all_gather(hidden, "col", axis=0, tiled=True), output_rows),
    )
    grad_input = lax.psum_scatter(partial_input, "row", scatter_dimension=0, tiled=True)
    factor = 1.0 / math.sqrt(input_cols.shape[0])
    return (grad_input, grad_gate * factor, grad_up * factor, grad_down * factor)


def solution(mesh):
    placed = (
        P("row", "col"),
        P("row", "col"),
        P("col", "row"),
        P("col", "row"),
        P("row", "col"),
        P("row", "col"),
        P("row", "col"),
    )
    return jax.shard_map(
        shards,
        mesh=mesh,
        in_specs=placed,
        out_specs=(P("row", "col"), P("row", "col"), P("row", "col"), P("row", "col")),
        check_vma=False,
    )
```

profile of v0, /device:TPU:8, one launch (start us, length us, event | category | flops | bytes accessed | tf_op | source)
XLA Modules:
  0.0 645.6 jit_solution(3945084945116645436)
XLA Ops:
  7.2 0.0 copy-start
  7.2 0.0 all-gather.6.cloned.1.call-start
  7.2 0.7 all-gather.6.cloned.1.call-update
  7.9 0.0 reduce-scatter.3.cloned.1.call-start
  8.0 55.2 %all-gather.6.cloned.1.call-done = bf16[2048,256]{1,0:T(8,128)(2,1)} async-done(((bf16[128,256]{1,0:T(8,128)(2,1)}), bf16[2048,256]{1,0:T(8,128)(2,1)}) %all-gather.6.cloned.1.call-update) | async-done | bytes 1048592 | tf_op jit(solution)/shard_map/all_gather | solution.py:23
  63.2 0.0 copy-done
  63.2 5.5 fusion.8
  68.6 0.0 copy-start.5
  68.6 0.0 copy-start.6
  68.6 0.0 copy-start.4
  68.6 0.0 reduce-scatter.3.cloned.1.call-update
  68.7 0.0 all-gather.8.cloned.1.call-start
  68.7 161.0 %reduce-scatter.3.cloned.1.call-done = f32[128,896]{1,0:T(8,128)} async-done(((f32[2048,896]{1,0:T(8,128)}), f32[128,896]{1,0:T(8,128)}) %reduce-scatter.3.cloned.1.call-update) | async-done | bytes 458768 | tf_op jit(solution)/shard_map/reduce_scatter | solution.py:31
  229.7 0.0 copy-done.5
  229.7 0.0 copy-done.6
  229.7 2.1 multiply_convert_fusion
  231.8 0.0 all-gather.8.cloned.1.call-update
  231.8 0.0 all-gather.10.cloned.1.call-start
  231.8 0.5 all-gather.10.cloned.1.call-update
  232.4 0.0 all-gather.12.cloned.1.call-start
  232.4 0.5 all-gather.12.cloned.1.call-update
  233.0 0.0 all-gather.14.cloned.1.call-start
  233.0 0.5 all-gather.14.cloned.1.call-update
  233.5 0.0 copy-start.3
  233.5 0.0 reduce-scatter.5.cloned.1.call-start
  233.6 89.1 %all-gather.8.cloned.1.call-done = bf16[2048,896]{1,0:T(8,128)(2,1)} async-done(((bf16[128,896]{1,0:T(8,128)(2,1)}), bf16[2048,896]{1,0:T(8,128)(2,1)}) %all-gather.8.cloned.1.call-update) | async-done | bytes 3670032 | tf_op jit(solution)/shard_map/all_gather | solution.py:38
  322.7 0.0 copy-done.4
  322.7 3.3 fusion.9
  326.0 88.2 %all-gather.10.cloned.1.call-done = bf16[2048,896]{1,0:T(8,128)(2,1)} async-done(((bf16[128,896]{1,0:T(8,128)(2,1)}), bf16[2048,896]{1,0:T(8,128)(2,1)}) %all-gather.10.cloned.1.call-update) | async-done | bytes 3670032 | tf_op jit(solution)/shard_map/all_gather | solution.py:39
  414.2 0.0 copy-done.3
  414.2 4.7 convolution_add_fusion
  418.9 0.0 reduce-scatter.5.cloned.1.call-update
  418.9 46.7 %all-gather.12.cloned.1.call-done = bf16[2048,256]{1,0:T(8,128)(2,1)} async-done(((bf16[128,256]{1,0:T(8,128)(2,1)}), bf16[2048,256]{1,0:T(8,128)(2,1)}) %all-gather.12.cloned.1.call-update) | async-done | bytes 1048592 | tf_op jit(solution)/shard_map/all_gather | solution.py:22
  465.6 0.0 copy-start.1
  465.6 0.0 copy-start.7
  465.6 4.6 convolution_multiply_fusion.1
  470.2 0.0 copy-done.1
  470.2 0.0 copy-done.7
  470.2 0.0 copy-start.2
  470.2 2.1 convolution_multiply_fusion.2
  472.3 84.0 %all-gather.14.cloned.1.call-done = bf16[2048,896]{1,0:T(8,128)(2,1)} async-done(((bf16[128,896]{1,0:T(8,128)(2,1)}), bf16[2048,896]{1,0:T(8,128)(2,1)}) %all-gather.14.cloned.1.call-update) | async-done | bytes 3670032 | tf_op jit(solution)/shard_map/all_gather | solution.py:49
  556.3 0.0 copy-done.2
  556.3 4.1 convolution_multiply_fusion
  560.4 78.3 %reduce-scatter.5.cloned.1.call-done = f32[128,256]{1,0:T(8,128)} async-done(((f32[2048,256]{1,0:T(8,128)}), f32[128,256]{1,0:T(8,128)}) %reduce-scatter.5.cloned.1.call-update) | async-done | bytes 131088 | tf_op jit(solution)/shard_map/reduce_scatter | solution.py:51
Async XLA Ops:
  7.2 56.0 %copy-start = (bf16[896,256]{1,0:T(8,128)(2,1)S(1)}, bf16[896,256]{1,0:T(8,128)(2,1)}, u32[]{:S(2)}) copy-start(bf16[896,256]{1,0:T(8,128)(2,1)} %param.13) | copy-start | bytes 1376260
  7.2 56.0 %all-gather.6.cloned.1.call-start = ((), (), s32[]{:S(2)}) async-start(), calls=%async_computation.2 | async-start | bytes 1114112 | tf_op jit(solution)/shard_map/all_gather | solution.py:23
  7.9 221.8 %reduce-scatter.3.cloned.1.call-start = ((), (), s32[]{:S(2)}) async-start(), calls=%async_computation.3 | async-start | bytes 7798784 | tf_op jit(solution)/shard_map/reduce_scatter | solution.py:31
  68.6 161.0 %copy-start.5 = (bf16[128,896]{1,0:T(8,128)(2,1)S(1)}, bf16[128,896]{1,0:T(8,128)(2,1)}, u32[]{:S(2)}) copy-start(bf16[128,896]{1,0:T(8,128)(2,1)} %param.9) | copy-start | bytes 688132
  68.6 161.0 %copy-start.6 = (bf16[128,896]{1,0:T(8,128)(2,1)S(1)}, bf16[128,896]{1,0:T(8,128)(2,1)}, u32[]{:S(2)}) copy-start(bf16[128,896]{1,0:T(8,128)(2,1)} %param.10) | copy-start | bytes 688132
  68.6 254.1 %copy-start.4 = (bf16[896,256]{1,0:T(8,128)(2,1)S(1)}, bf16[896,256]{1,0:T(8,128)(2,1)}, u32[]{:S(2)}) copy-start(bf16[896,256]{1,0:T(8,128)(2,1)} %param.11) | copy-start | bytes 1376260
  68.7 254.0 %all-gather.8.cloned.1.call-start = ((), (), s32[]{:S(2)}) async-start(), calls=%async_computation.4 | async-start | bytes 3899392 | tf_op jit(solution)/shard_map/all_gather | solution.py:38
  231.8 182.4 %all-gather.10.cloned.1.call-start = ((), (), s32[]{:S(2)}) async-start(), calls=%async_computation.5 | async-start | bytes 3899392 | tf_op jit(solution)/shard_map/all_gather | solution.py:39
  232.4 233.3 %all-gather.12.cloned.1.call-start = ((), (), s32[]{:S(2)}) async-start(), calls=%async_computation.7 | async-start | bytes 1114112 | tf_op jit(solution)/shard_map/all_gather | solution.py:22
  233.0 323.4 %all-gather.14.cloned.1.call-start = ((), (), s32[]{:S(2)}) async-start(), calls=%async_computation.8 | async-start | bytes 3899392 | tf_op jit(solution)/shard_map/all_gather | solution.py:49
  233.5 180.6 %copy-start.3 = (bf16[896,256]{1,0:T(8,128)(2,1)S(1)}, bf16[896,256]{1,0:T(8,128)(2,1)}, u32[]{:S(2)}) copy-start(bf16[896,256]{1,0:T(8,128)(2,1)} %param.12) | copy-start | bytes 1376260
  233.5 405.2 %reduce-scatter.5.cloned.1.call-start = ((), (), s32[]{:S(2)}) async-start(), calls=%async_computation.6 | async-start | bytes 2228224 | tf_op jit(solution)/shard_map/reduce_scatter | solution.py:51
  465.6 4.6 copy-start.1
  465.6 4.6 copy-start.7
  470.2 86.1 %copy-start.2 = (bf16[2048,256]{1,0:T(8,128)(2,1)S(1)}, bf16[2048,256]{1,0:T(8,128)(2,1)}, u32[]{:S(2)}) copy-start(bf16[2048,256]{1,0:T(8,128)(2,1)} %all-gather.6.cloned.1.call-done) | copy-start | bytes 3145732
Sparse Core Ops, SparseCore 0:
  10.8 52.3 all-gather.5
  68.8 160.8 reduce-scatter.2
  232.0 90.5 all-gather.7
  324.9 89.2 all-gather.9
  416.8 48.8 all-gather.11
  467.3 88.9 all-gather.13
  561.1 77.6 reduce-scatter.4
where the time goes:
time: 646 us
  waiting for transfers between devices  605 us (94%)
  matrix products  24.2 us (4%)
  between operations  14.2 us (2%)
    reduce_scatter x1, waiting for transfers between devices, shards(): lax.psum_scatter(inner_last(output_rows, down_weight), 'col', scatter_dim...  161 us
    all_gather x1, waiting for transfers between devices, shards(): gate_piece = lax.all_gather(grad_gate_pre, 'col', axis=0, tiled=True)  89.1 us
    all_gather x1, waiting for transfers between devices, shards(): up_piece = lax.all_gather(grad_up_pre, 'col', axis=0, tiled=True)  88.2 us
    all_gather x1, waiting for transfers between devices, shards(): lax.all_gather(hidden, 'col', axis=0, tiled=True)  84 us
    reduce_scatter x1, waiting for transfers between devices, shards(): lax.psum_scatter(partial_input, 'row', scatter_dimension=0, tiled=True)  78.3 us
    all_gather x1, waiting for transfers between devices, shards(): lax.all_gather(grad_output, 'row', axis=0, tiled=True)  55.2 us
    all_gather x1, waiting for transfers between devices, shards(): lax.all_gather(inputs, 'row', axis=0, tiled=True)  46.7 us
  transfers between devices with their start and end apart: 7, of which 7 were waited for; matrix products, arithmetic and copies ran while one was open for 3% of the time, Pallas kernels for 0%

commit v1 on v0

--- a/solution.py
+++ b/solution.py
@@ -36,7 +36,10 @@
     ).astype(jnp.bfloat16)
     grad_up_pre = (grad_hidden * silu_gate).astype(jnp.bfloat16)
     gate_piece = lax.all_gather(grad_gate_pre, "col", axis=0, tiled=True)
-    up_piece = lax.all_gather(grad_up_pre, "col", axis=0, tiled=True)
+    size = lax.axis_size("col")
+    pieces = jnp.stack([grad_up_pre for _ in range(size)])
+    pieces = lax.all_to_all(pieces, "col", split_axis=0, concat_axis=0)
+    up_piece = jnp.concatenate(pieces, axis=0)
     gate_running = outer_sum(gate_piece, input_cols)
     up_running = outer_sum(up_piece, input_cols)
     input_part = jnp.dot(gate_piece, gate_weight, preferred_element_type=jnp.float32) + jnp.dot(

time: 646 us -> 617 us (0.955)
  waiting for transfers between devices: 605 us -> 566 us
  starting transfers between devices: 0.27 us -> 7.48 us
    all_gather x1 -> x0, waiting for transfers between devices: 88.2 us -> none  [shards(): up_piece = lax.all_gather(grad_up_pre, 'col', axis=0, tiled=True)]
    all_gather x1, waiting for transfers between devices: 89.1 us -> 141 us  [shards(): gate_piece = lax.all_gather(grad_gate_pre, 'col', axis=0, tiled=True)]
    all_to_all x0 -> x1, starting transfers between devices: none -> 7.24 us  [shards(): pieces = lax.all_to_all(pieces, 'col', split_axis=0, concat_axis=0)]
  transfers between devices with their start and end apart: 7 -> 7, of which waited for: 7 -> 6; matrix products, arithmetic and copies ran while one was open for 3% -> 3% of each run, Pallas kernels for 0% -> 0%
where the time goes in v1:
time: 617 us; the launch traced here: 616 us
  waiting for transfers between devices  566 us (92%)
  matrix products  24.2 us (4%)
  between operations  14.2 us (2%)
  starting transfers between devices  7.48 us (1%)
    reduce_scatter x1, waiting for transfers between devices, shards(): lax.psum_scatter(inner_last(output_rows, down_weight), 'col', scatter_dim...  161 us
    all_gather x1, waiting for transfers between devices, shards(): gate_piece = lax.all_gather(grad_gate_pre, 'col', axis=0, tiled=True)  141 us
    all_gather x1, waiting for transfers between devices, shards(): lax.all_gather(hidden, 'col', axis=0, tiled=True)  84 us
    reduce_scatter x1, waiting for transfers between devices, shards(): lax.psum_scatter(partial_input, 'row', scatter_dimension=0, tiled=True)  78.2 us
    all_gather x1, waiting for transfers between devices, shards(): lax.all_gather(grad_output, 'row', axis=0, tiled=True)  55.2 us
    all_gather x1, waiting for transfers between devices, shards(): lax.all_gather(inputs, 'row', axis=0, tiled=True)  44.5 us
  transfers between devices with their start and end apart: 7, of which 6 were waited for; matrix products, arithmetic and copies ran while one was open for 3% of the time, Pallas kernels for 0%

profile of v1, /device:TPU:8, one launch (start us, length us, event | category | flops | bytes accessed | tf_op | source)
XLA Modules:
  0.0 616.5 jit_solution(11039970918786801526)
XLA Ops:
  7.2 0.0 copy-start
  7.2 0.0 all-gather.5.cloned.1.call-start
  7.2 0.7 all-gather.5.cloned.1.call-update
  7.9 0.0 reduce-scatter.3.cloned.1.call-start
  8.0 55.2 %all-gather.5.cloned.1.call-done = bf16[2048,256]{1,0:T(8,128)(2,1)} async-done(((bf16[128,256]{1,0:T(8,128)(2,1)}), bf16[2048,256]{1,0:T(8,128)(2,1)}) %all-gather.5.cloned.1.call-update) | async-done | bytes 1048592 | tf_op jit(solution)/shard_map/all_gather | solution.py:23
  63.2 0.0 copy-done
  63.2 5.5 fusion.8
  68.6 0.0 copy-start.5
  68.6 0.0 copy-start.6
  68.6 0.0 reduce-scatter.3.cloned.1.call-update
  68.7 0.0 all-gather.7.cloned.1.call-start
  68.7 161.0 %reduce-scatter.3.cloned.1.call-done = f32[128,896]{1,0:T(8,128)} async-done(((f32[2048,896]{1,0:T(8,128)}), f32[128,896]{1,0:T(8,128)}) %reduce-scatter.3.cloned.1.call-update) | async-done | bytes 458768 | tf_op jit(solution)/shard_map/reduce_scatter | solution.py:31
  229.7 0.0 copy-done.5
  229.7 0.0 copy-done.6
  229.7 2.1 multiply_convert_fusion
  231.7 0.0 all-gather.7.cloned.1.call-update
  231.8 0.0 all-gather.9.cloned.1.call-start
  231.8 0.5 all-gather.9.cloned.1.call-update
  232.3 2.4 stack.2
  234.8 0.0 copy-start.4
  234.8 7.2 %all-to-all-start = ((bf16[16,128,896]{2,1,0:T(8,128)(2,1)}), bf16[16,128,896]{2,1,0:T(8,128)(2,1)}, u32[]{:S(2)}, u32[]{:S(2)}) async-start(bf16[16,128,896]{2,1,0:T(8,128)(2,1)} %stack.2), calls=%async_computation.1 | async-start | bytes 7340032 | tf_op jit(solution)/shard_map/all_to_all | solution.py:41
  242.0 0.0 all-gather.11.cloned.1.call-start
  242.1 0.5 all-gather.11.cloned.1.call-update
  242.6 0.0 copy-start.3
  242.6 0.0 reduce-scatter.5.cloned.1.call-start
  242.7 141.5 %all-gather.7.cloned.1.call-done = bf16[2048,896]{1,0:T(8,128)(2,1)} async-done(((bf16[128,896]{1,0:T(8,128)(2,1)}), bf16[2048,896]{1,0:T(8,128)(2,1)}) %all-gather.7.cloned.1.call-update) | async-done | bytes 3670032 | tf_op jit(solution)/shard_map/all_gather | solution.py:38
  384.1 0.0 copy-done.4
  384.1 3.3 fusion.9
  387.4 0.0 all-to-all-done
  387.4 0.0 copy-done.3
  387.5 4.7 convolution_add_fusion
  392.2 0.0 reduce-scatter.5.cloned.1.call-update
  392.2 44.5 %all-gather.9.cloned.1.call-done = bf16[2048,256]{1,0:T(8,128)(2,1)} async-done(((bf16[128,256]{1,0:T(8,128)(2,1)}), bf16[2048,256]{1,0:T(8,128)(2,1)}) %all-gather.9.cloned.1.call-update) | async-done | bytes 1048592 | tf_op jit(solution)/shard_map/all_gather | solution.py:22
  436.7 0.0 copy-start.1
  436.7 0.0 copy-start.7
  436.7 4.6 convolution_multiply_fusion.1
  441.2 0.0 copy-done.1
  441.2 0.0 copy-done.7
  441.2 0.0 copy-start.2
  441.2 2.1 convolution_multiply_fusion.2
  443.3 84.0 %all-gather.11.cloned.1.call-done = bf16[2048,896]{1,0:T(8,128)(2,1)} async-done(((bf16[128,896]{1,0:T(8,128)(2,1)}), bf16[2048,896]{1,0:T(8,128)(2,1)}) %all-gather.11.cloned.1.call-update) | async-done | bytes 3670032 | tf_op jit(solution)/shard_map/all_gather | solution.py:52
  527.3 0.0 copy-done.2
  527.3 4.1 convolution_multiply_fusion
  531.5 78.2 %reduce-scatter.5.cloned.1.call-done = f32[128,256]{1,0:T(8,128)} async-done(((f32[2048,256]{1,0:T(8,128)}), f32[128,256]{1,0:T(8,128)}) %reduce-scatter.5.cloned.1.call-update) | async-done | bytes 131088 | tf_op jit(solution)/shard_map/reduce_scatter | solution.py:54
Async XLA Ops:
  7.2 56.0 %copy-start = (bf16[896,256]{1,0:T(8,128)(2,1)S(1)}, bf16[896,256]{1,0:T(8,128)(2,1)}, u32[]{:S(2)}) copy-start(bf16[896,256]{1,0:T(8,128)(2,1)} %param.13) | copy-start | bytes 1376260
  7.2 56.0 %all-gather.5.cloned.1.call-start = ((), (), s32[]{:S(2)}) async-start(), calls=%async_computation.3 | async-start | bytes 1114112 | tf_op jit(solution)/shard_map/all_gather | solution.py:23
  7.9 221.8 %reduce-scatter.3.cloned.1.call-start = ((), (), s32[]{:S(2)}) async-start(), calls=%async_computation.4 | async-start | bytes 7798784 | tf_op jit(solution)/shard_map/reduce_scatter | solution.py:31
  68.6 161.0 %copy-start.5 = (bf16[128,896]{1,0:T(8,128)(2,1)S(1)}, bf16[128,896]{1,0:T(8,128)(2,1)}, u32[]{:S(2)}) copy-start(bf16[128,896]{1,0:T(8,128)(2,1)} %param.9) | copy-start | bytes 688132
  68.6 161.0 %copy-start.6 = (bf16[128,896]{1,0:T(8,128)(2,1)S(1)}, bf16[128,896]{1,0:T(8,128)(2,1)}, u32[]{:S(2)}) copy-start(bf16[128,896]{1,0:T(8,128)(2,1)} %param.10) | copy-start | bytes 688132
  68.7 315.5 %all-gather.7.cloned.1.call-start = ((), (), s32[]{:S(2)}) async-start(), calls=%async_computation.5 | async-start | bytes 3899392 | tf_op jit(solution)/shard_map/all_gather | solution.py:38
  231.8 204.9 %all-gather.9.cloned.1.call-start = ((), (), s32[]{:S(2)}) async-start(), calls=%async_computation.7 | async-start | bytes 1114112 | tf_op jit(solution)/shard_map/all_gather | solution.py:22
  234.8 149.4 %copy-start.4 = (bf16[896,256]{1,0:T(8,128)(2,1)S(1)}, bf16[896,256]{1,0:T(8,128)(2,1)}, u32[]{:S(2)}) copy-start(bf16[896,256]{1,0:T(8,128)(2,1)} %param.11) | copy-start | bytes 1376260
  234.8 152.7 %all-to-all-start = ((bf16[16,128,896]{2,1,0:T(8,128)(2,1)}), bf16[16,128,896]{2,1,0:T(8,128)(2,1)}, u32[]{:S(2)}, u32[]{:S(2)}) async-start(bf16[16,128,896]{2,1,0:T(8,128)(2,1)} %stack.2), calls=%async_computation.1 | async-start | bytes 7340032 | tf_op jit(solution)/shard_map/all_to_all | solution.py:41
  242.0 285.3 %all-gather.11.cloned.1.call-start = ((), (), s32[]{:S(2)}) async-start(), calls=%async_computation.8 | async-start | bytes 3899392 | tf_op jit(solution)/shard_map/all_gather | solution.py:52
  242.6 144.8 %copy-start.3 = (bf16[896,256]{1,0:T(8,128)(2,1)S(1)}, bf16[896,256]{1,0:T(8,128)(2,1)}, u32[]{:S(2)}) copy-start(bf16[896,256]{1,0:T(8,128)(2,1)} %param.12) | copy-start | bytes 1376260
  242.6 367.0 %reduce-scatter.5.cloned.1.call-start = ((), (), s32[]{:S(2)}) async-start(), calls=%async_computation.6 | async-start | bytes 2228224 | tf_op jit(solution)/shard_map/reduce_scatter | solution.py:54
  436.7 4.6 copy-start.1
  436.7 4.6 copy-start.7
  441.2 86.1 %copy-start.2 = (bf16[2048,256]{1,0:T(8,128)(2,1)S(1)}, bf16[2048,256]{1,0:T(8,128)(2,1)}, u32[]{:S(2)}) copy-start(bf16[2048,256]{1,0:T(8,128)(2,1)} %all-gather.5.cloned.1.call-done) | copy-start | bytes 3145732
Sparse Core Ops, SparseCore 0:
  10.8 52.3 all-gather.4
  68.8 160.8 reduce-scatter.2
  232.0 152.0 all-gather.6
  386.8 49.8 all-gather.8
  438.3 88.9 all-gather.10
  531.9 77.6 reduce-scatter.4
